TPU v7x, 32 devices: a whole 2x2x4 slice. The times are simulated.
32 devices in a mesh: seq: 8 (over z, x), tp: 4 (over y, core).
Axes of the slice: x: 2, y: 2, z: 4, core: 2. Of those that a mesh axis runs over, the one named last changes fastest.
Arguments:
- queries: bfloat16 [4096, 4096], P('seq', 'tp'), may hold values from -6 to 6
- keys: bfloat16 [4096, 4096], P('seq', 'tp'), may hold values from -6 to 6
- values: bfloat16 [4096, 4096], P('seq', 'tp'), may hold values from -6 to 6
- log_decay: float32 [4096, 32], P('seq', 'tp'), may hold values from -1.2 to 0, as said below
- out_weight: bfloat16 [4096, 6144], P('tp', 'seq'), may hold values from -0.09375 to 0.09375
- grad_out: bfloat16 [4096, 6144], P('seq', 'tp'), may hold values from -6 to 6
Outputs:
- grad_queries: bfloat16 [4096, 4096], P('seq', 'tp')
- grad_keys: bfloat16 [4096, 4096], P('seq', 'tp')
- grad_values: bfloat16 [4096, 4096], P('seq', 'tp')
- grad_weight: float32 [6144, 4096], P('seq', 'tp')
Inputs may be any that keep to these rules, and one draw needn't show every extreme that they name: `log_decay`: log decay of each head's state at each token.
All inputs are finite; a program needn't handle non-finite values.
Results may differ from a plain program's by a relative error of at most 0.0029.
Values may be sent and summed in bfloat16 or wider, within the bound.
A program may use at most 192 MiB of HBM per device.

v0:
```python
import jax
import jax.numpy as jnp
from jax import lax
from jax.sharding import PartitionSpec as P

BLOCK = 256
EPS = 1e-06
HIGH = lax.Precision.HIGHEST


def carried_in(value, axis, join, neutral, backward):
    count, mine = (lax.axis_size(axis), lax.axis_index(axis))
    pieces = jax.tree.map(lambda part: lax.all_gather(part, axis), value)
    if backward:
        pieces = jax.tree.map(lambda part: part[::-1], pieces)
        mine = count - 1 - mine
    total = jax.tree.map(
        lambda part, zero: jnp.full_like(part, 0) + jnp.asarray(zero, part.dtype), value, neutral
    )

    def turn(position, total):
        longer = join(total, jax.tree.map(lambda part: part[position], pieces))
        return jax.tree.map(lambda new, old: jnp.where(position < mine, new, old), longer, total)

    return lax.fori_loop(0, count - 1, turn, total)


def chain(earlier, later):
    log_early, state_early = earlier
    log_late, state_late = later
    return (log_early + log_late, jnp.exp(log_late)[:, None, None] * state_early + state_late)


def on_device(queries, keys, values, log_decay, out_weight, grad_out):
    tok_rows = queries.shape[0]
    heads_here = log_decay.shape[1]
    head_size = queries.shape[1] // heads_here
    blocks = tok_rows // BLOCK
    shape4 = (blocks, BLOCK, heads_here, head_size)
    query_b = queries.reshape(shape4)
    key_b = keys.reshape(shape4)
    query_f = queries.astype(jnp.float32).reshape(shape4)
    key_f = keys.astype(jnp.float32).reshape(shape4)
    value_f = values.astype(jnp.float32).reshape(shape4)
    rates = log_decay.reshape(blocks, BLOCK, heads_here)
    cumul = jnp.cumsum(rates, axis=1)
    totals = cumul[:, -1, :]
    running = jnp.cumsum(totals, axis=0)
    before = running - totals
    dev_log = running[-1]
    cumul_t = jnp.transpose(cumul, (0, 2, 1))
    lower = jnp.arange(BLOCK)[:, None] >= jnp.arange(BLOCK)[None, :]
    decay_mat = jnp.where(
        lower[None, None],
        jnp.exp(jnp.minimum(cumul_t[:, :, :, None] - cumul_t[:, :, None, :], 0.0)),
        0.0,
    )
    scores = (
        jnp.einsum("nthd,nshd->nhts", query_b, key_b, preferred_element_type=jnp.float32)
        * decay_mat
    )
    into_end = jnp.exp(totals[:, None, :] - cumul)
    from_start = jnp.exp(cumul)
    block_states = jnp.einsum("nth,nthd,nthe->nhde", into_end, key_f, value_f, precision=HIGH)
    order = jnp.arange(blocks)
    earlier_mask = order[None, :] < order[:, None]
    forward_mix = jnp.where(
        earlier_mask[:, :, None],
        jnp.exp(jnp.minimum(before[:, None, :] - running[None, :, :], 0.0)),
        0.0,
    )
    prefix_local = jnp.einsum("nmh,mhde->nhde", forward_mix, block_states, precision=HIGH)
    dev_state = jnp.einsum(
        "mh,mhde->hde", jnp.exp(dev_log[None, :] - running), block_states, precision=HIGH
    )
    zero_log = jnp.zeros_like(dev_log)
    zero_state = jnp.zeros_like(dev_state)
    state_in = carried_in((dev_log, dev_state), "seq", chain, (zero_log, zero_state), False)[1]
    start_states = prefix_local + jnp.exp(before)[:, :, None, None] * state_in[None]
    attended = jnp.einsum("nhts,nshd->nthd", scores, value_f, precision=HIGH)
    attended = attended + from_start[..., None] * jnp.einsum(
        "nthd,nhde->nthe", query_f, start_states, precision=HIGH
    )
    scale = jnp.sqrt(jnp.mean(attended * attended, axis=-1, keepdims=True) + EPS)
    o_hat = attended / scale
    normed = o_hat.reshape(tok_rows, -1).astype(jnp.bfloat16)
    cotangent = lax.all_gather(grad_out, "tp", axis=1, tiled=True)
    grad_normed = lax.dot_general(
        cotangent,
        lax.all_gather(out_weight, "seq", axis=1, tiled=True),
        (((1,), (1,)), ((), ())),
        preferred_element_type=jnp.float32,
    )
    grad_hat = grad_normed.reshape(shape4)
    grad_att = (grad_hat - o_hat * jnp.mean(grad_hat * o_hat, axis=-1, keepdims=True)) / scale
    grad_mix = jnp.einsum("nthe,nshe->nhts", grad_att, value_f, precision=HIGH) * decay_mat
    grad_q = jnp.einsum("nhts,nshd->nthd", grad_mix, key_f, precision=HIGH)
    grad_q = grad_q + from_start[..., None] * jnp.einsum(
        "nthe,nhde->nthd", grad_att, start_states, precision=HIGH
    )
    block_grads = jnp.einsum("nth,nthd,nthe->nhde", from_start, query_f, grad_att, precision=HIGH)
    later_mask = order[None, :] > order[:, None]
    backward_mix = jnp.where(
        later_mask[:, :, None],
        jnp.exp(jnp.minimum(before[None, :, :] - running[:, None, :], 0.0)),
        0.0,
    )
    suffix_local = jnp.einsum("nmh,mhde->nhde", backward_mix, block_grads, precision=HIGH)
    dev_grad = jnp.einsum("mh,mhde->hde", jnp.exp(before), block_grads, precision=HIGH)
    grad_in = carried_in((dev_log, dev_grad), "seq", chain, (zero_log, zero_state), True)[1]
    end_grads = suffix_local + jnp.exp(dev_log[None, :] - running)[:, :, None, None] * grad_in[None]
    grad_k = jnp.einsum("nhts,nthd->nshd", grad_mix, query_f, precision=HIGH)
    grad_k = grad_k + into_end[..., None] * jnp.einsum(
        "nthe,nhde->nthd", value_f, end_grads, precision=HIGH
    )
    grad_v = jnp.einsum("nhts,nthe->nshe", scores, grad_att, precision=HIGH)
    grad_v = grad_v + into_end[..., None] * jnp.einsum(
        "nthd,nhde->nthe", key_f, end_grads, precision=HIGH
    )
    by_columns = lax.all_to_all(cotangent, "seq", split_axis=1, concat_axis=0, tiled=True)
    grad_weight = lax.dot_general(
        by_columns,
        lax.all_gather(normed, "seq", axis=0, tiled=True),
        (((0,), (0,)), ((), ())),
        preferred_element_type=jnp.float32,
    )
    return (
        grad_q.reshape(tok_rows, -1).astype(jnp.bfloat16),
        grad_k.reshape(tok_rows, -1).astype(jnp.bfloat16),
        grad_v.reshape(tok_rows, -1).astype(jnp.bfloat16),
        grad_weight,
    )


def solution(mesh):
    placed = (
        P("seq", "tp"),
        P("seq", "tp"),
        P("seq", "tp"),
        P("seq", "tp"),
        P("tp", "seq"),
        P("seq", "tp"),
    )
    return jax.shard_map(
        on_device,
        mesh=mesh,
        in_specs=placed,
        out_specs=(P("seq", "tp"), P("seq", "tp"), P("seq", "tp"), P("seq", "tp")),
        check_vma=False,
    )
```

profile of v0, /device:TPU:0, one launch (start us, length us, event | category | flops | bytes accessed | tf_op | source)
XLA Modules:
  0.0 677.9 jit_solution(5137441906326079839)
XLA Ops:
  17.3 4.4 fusion.47
  27.6 22.4 %all-gather.2 = f32[8,1,8]{2,1,0:T(1,128)S(1)} all-gather(f32[1,1,8]{2,1,0:T(1,128)S(1)} %get-tuple-element.278), channel_id=1, replica_groups=mesh['seq'=8,'tp'=4] {'seq'}, dimensions={0}, use_global_device_ids=true | all-gather | bytes 288 | tf_op jit(solution)/shard_map/all_gather | solution.py:13
  50.0 6.3 fusion.49
  60.4 5.0 fusion.6
  65.4 32.6 %all-gather.15.cloned.1.call-done = f32[64,128,128]{2,1,0:T(8,128)} async-done(((f32[8,128,128]{2,1,0:T(8,128)}), f32[64,128,128]{2,1,0:T(8,128)}) %all-gather.15.cloned.1.call-update) | async-done | bytes 4194320 | tf_op jit(solution)/shard_map/all_gather | solution.py:13
  98.0 8.7 %while.28 = (s32[]{:T(128)}, f32[8,128,128]{2,1,0:T(8,128)S(1)}, s32[]{:T(128)}, f32[8,8]{1,0:T(8,128)S(1)}, f32[8,8,128,128]{3,2,1,0:T(8,128)}, /*index=5*/s32[]{:T(128)}, s32[]{:T(128)}) while((s32[]{:T(128)}, f32[8,128,128]{2,1,0:T(8,128)S(1)}, s32[]{:T(128)}, f32[8,8]{1,0:T(8,128)S(1)}, f32[8,8,128,128]{3,2,1,0:T(8,128)}, ...), condition=%wide.region_4.5_spmd.clone, body=%wide.region_3.4_spmd.clone.sunk | while | flops 524292 | bytes 1573073 | solution.py:25
  106.7 4.5 multiply_reduce_fusion.1
  111.2 33.0 %all-gather.9.cloned.1.call-done = bf16[512,6144]{0,1:T(8,128)(2,1)} async-done(((bf16[512,1536]{0,1:T(8,128)(2,1)}), bf16[512,6144]{0,1:T(8,128)(2,1)}) %all-gather.9.cloned.1.call-update) | async-done | bytes 6291472 | tf_op jit(solution)/shard_map/all_gather | solution.py:87
  144.2 178.5 %all-gather.11.cloned.1.call-done = bf16[1024,6144]{1,0:T(8,128)(2,1)} async-done(((bf16[1024,768]{1,0:T(8,128)(2,1)}), bf16[1024,6144]{1,0:T(8,128)(2,1)}) %all-gather.11.cloned.1.call-update) | async-done | bytes 12582928 | tf_op jit(solution)/shard_map/all_gather | solution.py:90
  322.7 11.5 %convolution_bitcast_fusion.1 = f32[64,8,8,128]{3,1,2,0:T(8,128)S(1)} fusion(bf16[512,6144]{0,1:T(8,128)(2,1)} %all-gather.9.cloned.1.call-done, bf16[1024,6144]{1,0:T(8,128)(2,1)} %all-gather.11.cloned.1.call-done), kind=kOutput, calls=%fused_computation.50 | convolution fusion | flops 6442450944 | bytes 20971520 | tf_op jit(solution)/shard_map/dot_general | solution.py:88
  347.5 4.6 fusion.43
  352.2 4.8 all-to-all-start
  362.1 193.0 %all-to-all-done = bf16[512,8,768]{0,2,1:T(8,128)(2,1)} async-done(((bf16[512,8,768]{0,2,1:T(8,128)(2,1)}), bf16[512,8,768]{0,2,1:T(8,128)(2,1)}, u32[]{:S(2)}, u32[]{:S(2)}) %all-to-all-start) | async-done | bytes 6291488 | tf_op jit(solution)/shard_map/all_to_all | solution.py:120
  555.1 8.6 %copy.211 = bf16[8,512,768]{2,1,0:T(8,128)(2,1)} copy(bf16[8,512,768]{1,2,0:T(8,128)(2,1)} %bitcast.34) | data formatting | bytes 12582912 | tf_op jit(solution)/shard_map/all_to_all | solution.py:120
  563.7 3.2 fusion.53
  567.0 3.7 fusion.10
  579.2 6.3 fusion.45
  585.6 8.0 %fusion.8 = f32[2,8,256,128]{3,2,1,0:T(8,128)} fusion(bf16[2,256,8,128]{1,3,2,0:T(8,128)(2,1)S(1)} %copy-done.6, f32[2,8,256,256]{3,2,1,0:T(8,128)} %copy-done.13, f32[2,8,256]{2,1,0:T(8,128)S(1)} %add_bitcast_fusion.1, pred[256,256]{1,0:T(8,128)(4,1)S(1)} %iota_compare_fusion), kind=kOutput, calls=%fused_computation.11 | convolution fusion | flops 1614807040 | bytes 7421952 | tf_op jit(solution)/shard_map/nhts,nthd->nshd/dot_general | solution.py:112
  593.6 9.2 %fusion.4 = f32[2,8,128,256]{2,3,1,0:T(8,128)} fusion(f32[2,256,8,128]{1,3,2,0:T(8,128)S(1)} %get-tuple-element.275, f32[2,8,256,256]{3,2,1,0:T(8,128)S(1)} %copy-done.3, f32[2,8,256]{2,1,0:T(8,128)S(1)} %add_bitcast_fusion.1, pred[256,256]{1,0:T(8,128)(4,1)S(1)} %iota_compare_fusion), kind=kOutput, calls=%fused_computation.9 | convolution fusion | flops 1614807040 | bytes 8470528 | tf_op jit(solution)/shard_map/nhts,nthe->nshe/dot_general | solution.py:116
  602.8 4.7 rev.7
  607.5 8.6 %while.29 = (s32[]{:T(128)}, f32[8,128,128]{2,1,0:T(8,128)S(1)}, s32[]{:T(128)}, f32[8,8]{1,0:T(8,128)S(1)}, f32[8,8,128,128]{3,2,1,0:T(8,128)}, /*index=5*/s32[]{:T(128)}, s32[]{:T(128)}) while((s32[]{:T(128)}, f32[8,128,128]{2,1,0:T(8,128)S(1)}, s32[]{:T(128)}, f32[8,8]{1,0:T(8,128)S(1)}, f32[8,8,128,128]{3,2,1,0:T(8,128)}, ...), condition=%wide.region_8.9_spmd.clone, body=%wide.region_7.8_spmd.clone.sunk | while | flops 524292 | bytes 1573073 | solution.py:25
  616.1 3.4 fusion.13
  624.5 33.3 %all-gather.13.cloned.1.call-done = bf16[4096,1024]{1,0:T(8,128)(2,1)} async-done(((bf16[512,1024]{1,0:T(8,128)(2,1)}), bf16[4096,1024]{1,0:T(8,128)(2,1)}) %all-gather.13.cloned.1.call-update) | async-done | bytes 8388624 | tf_op jit(solution)/shard_map/all_gather | solution.py:123
  657.8 11.0 %convolution_bitcast_fusion = f32[768,1024]{0,1:T(8,128)S(1)} fusion(bf16[4096,1024]{1,0:T(8,128)(2,1)} %all-gather.13.cloned.1.call-done, bf16[4096,768]{1,0:T(8,128)(2,1)} %bitcast.156), kind=kOutput, calls=%fused_computation.49 | convolution fusion | flops 6442450944 | bytes 17825792 | tf_op jit(solution)/shard_map/dot_general | solution.py:121
  (126 shorter events, 71.0 us)
Async XLA Ops:
  7.2 90.8 %all-gather.15.cloned.1.call-start = ((), (), s32[]{:S(2)}) async-start(), calls=%async_computation.4 | async-start | bytes 4718592 | tf_op jit(solution)/shard_map/all_gather | solution.py:13
  11.6 1.9 copy-start.10
  13.5 44.8 %copy-start.8 = (bf16[64,8,8,128]{3,2,1,0:T(8,128)(2,1)}, bf16[64,8,8,128]{3,2,1,0:T(8,128)(2,1)S(1)}, u32[]{:S(2)}) copy-start(bf16[64,8,8,128]{3,2,1,0:T(8,128)(2,1)S(1)} %copy.234) | copy-start | bytes 3145732
  13.5 8.3 %copy-start.16 = (bf16[512,1536]{1,0:T(8,128)(2,1)S(1)}, bf16[512,1536]{1,0:T(8,128)(2,1)}, u32[]{:S(2)}) copy-start(bf16[512,1536]{1,0:T(8,128)(2,1)} %param.15) | copy-start | bytes 4718596
  21.7 122.5 %all-gather.9.cloned.1.call-start = ((), (), s32[]{:S(2)}) async-start(), calls=%async_computation.1 | async-start | bytes 7864320 | tf_op jit(solution)/shard_map/all_gather | solution.py:87
  23.4 1.3 copy-start.18
  23.4 299.3 %all-gather.11.cloned.1.call-start = ((), (), s32[]{:S(2)}) async-start(), calls=%async_computation.2 | async-start | bytes 14155776 | tf_op jit(solution)/shard_map/all_gather | solution.py:90
  24.1 578.6 %all-gather.17.cloned.1.call-start = ((), (), s32[]{:S(2)}) async-start(), calls=%async_computation.5 | async-start | bytes 4718592 | tf_op jit(solution)/shard_map/all_gather | solution.py:13
  27.5 30.8 %copy-start.4 = (bf16[2,256,8,128]{1,3,2,0:T(8,128)(2,1)}, bf16[2,256,8,128]{1,3,2,0:T(8,128)(2,1)S(1)}, u32[]{:S(2)}) copy-start(bf16[2,256,8,128]{1,3,2,0:T(8,128)(2,1)S(1)} %copy.196) | copy-start | bytes 3145732
  58.3 2.0 copy-start.2
  111.2 227.7 %copy-start = (f32[2,256,8,128]{1,3,2,0:T(8,128)}, f32[2,256,8,128]{1,3,2,0:T(8,128)S(1)}, u32[]{:S(2)}) copy-start(f32[2,256,8,128]{1,3,2,0:T(8,128)S(1)} %get-tuple-element.280) | copy-start | bytes 6291460
  338.9 2.2 copy-start.1
  341.1 3.1 copy-start.5
  346.5 1.0 copy-start.14
  352.2 202.9 %all-to-all-start = ((bf16[512,8,768]{0,2,1:T(8,128)(2,1)}), bf16[512,8,768]{0,2,1:T(8,128)(2,1)}, u32[]{:S(2)}, u32[]{:S(2)}) async-start(bf16[512,8,768]{0,2,1:T(8,128)(2,1)} %bitcast.155), calls=%async_computation | async-start | bytes 12582912 | tf_op jit(solution)/shard_map/all_to_all | solution.py:120
  357.0 300.8 %all-gather.13.cloned.1.call-start = ((), (), s32[]{:S(2)}) async-start(), calls=%async_computation.3 | async-start | bytes 9437184 | tf_op jit(solution)/shard_map/all_gather | solution.py:123
  563.7 3.2 copy-start.11
  566.9 3.7 copy-start.13
  566.9 3.7 copy-start.12
  576.7 8.9 %copy-start.6 = (bf16[2,256,8,128]{1,3,2,0:T(8,128)(2,1)S(1)}, bf16[2,256,8,128]{1,3,2,0:T(8,128)(2,1)}, u32[]{:S(2)}) copy-start(bf16[2,256,8,128]{1,3,2,0:T(8,128)(2,1)} %copy-done.4) | copy-start | bytes 3145732
  585.5 8.0 %copy-start.3 = (f32[2,8,256,256]{3,2,1,0:T(8,128)S(1)}, f32[2,8,256,256]{3,2,1,0:T(8,128)}, u32[]{:S(2)}) copy-start(f32[2,8,256,256]{3,2,1,0:T(8,128)} %copy-done.2) | copy-start | bytes 12582916
  607.5 8.6 %copy-start.7 = (f32[8,128,128,2]{2,3,1,0:T(2,128)S(1)}, f32[8,128,128,2]{2,3,1,0:T(2,128)}, u32[]{:S(2)}) copy-start(f32[8,128,128,2]{2,3,1,0:T(2,128)} %fusion.45) | copy-start | bytes 3145732
  616.1 4.1 copy-start.9
  616.1 4.1 copy-start.15
  (1 other events, 1.0 us)
Sparse Core Ops, SparseCore 0:
  21.8 76.1 all-gather.14
  99.6 44.6 all-gather.8
  146.5 176.2 all-gather.10
  352.3 177.9 all-gather.16
  532.3 125.4 all-gather.12
where the time goes:
time: 687 us; the launch traced here: 678 us
  waiting for transfers between devices  471 us (69%)
  matrix products  93.1 us (14%)
  local copies, waits for them, and re-layouts  46.9 us (7%)
  other arithmetic  24.7 us (4%)
  blocking collectives  22.4 us (3%)
  between operations  14.4 us (2%)
    all_to_all x1, waiting for transfers between devices, on_device(): lax.all_to_all(cotangent, 'seq', split_axis=1, concat_axis=0, tiled=True)  193 us
    all_gather x1, waiting for transfers between devices, on_device(): lax.all_gather(out_weight, 'seq', axis=1, tiled=True)  178 us
    all_gather x1, waiting for transfers between devices, on_device(): lax.all_gather(normed, 'seq', axis=0, tiled=True)  33.3 us
    all_gather x1, waiting for transfers between devices, on_device(): cotangent = lax.all_gather(grad_out, 'tp', axis=1, tiled=True)  33 us
    all_gather x2, waiting for transfers between devices, carried_in(): pieces = jax.tree.map(lambda part: lax.all_gather(part, axis), value)  32.6 us
    all_gather x1, blocking collectives, carried_in(): pieces = jax.tree.map(lambda part: lax.all_gather(part, axis), value)  22.4 us
    unnamed x46, local copies, waits for them, and re-layouts  19.6 us
    select_n x14, other arithmetic, turn(): jnp.where(position < mine, new, old)  16.8 us
  transfers between devices with their start and end apart: 6, of which 5 were waited for; matrix products, arithmetic and copies ran while one was open for 16% of the time, Pallas kernels for 0%

commit v1 on v0

--- a/solution.py
+++ b/solution.py
@@ -84,7 +84,12 @@
     scale = jnp.sqrt(jnp.mean(attended * attended, axis=-1, keepdims=True) + EPS)
     o_hat = attended / scale
     normed = o_hat.reshape(tok_rows, -1).astype(jnp.bfloat16)
-    cotangent = lax.all_gather(grad_out, "tp", axis=1, tiled=True)
+    ring = [grad_out]
+    for hop in range(3):
+        ring.append(lax.ppermute(ring[-1], "tp", [(dev, (dev + 1) % 4) for dev in range(4)]))
+    cotangent = jnp.roll(
+        jnp.concatenate(ring[::-1], axis=1), (lax.axis_index("tp") + 1) * ring[0].shape[1], axis=1
+    )
     grad_normed = lax.dot_general(
         cotangent,
         lax.all_gather(out_weight, "seq", axis=1, tiled=True),

time: 687 us -> 639 us (0.930)
  waiting for transfers between devices: 471 us -> 415 us
  local copies, waits for them, and re-layouts: 46.9 us -> 55 us
    all_gather x1 -> x0, waiting for transfers between devices: 33 us -> none  [on_device(): cotangent = lax.all_gather(grad_out, 'tp', axis=1, tiled=True)]
    all_gather x2, waiting for transfers between devices: 32.6 us -> 0.01 us  [carried_in(): pieces = jax.tree.map(lambda part: lax.all_gather(part, axis), value)]
    ppermute x0 -> x3, waiting for transfers between devices: none -> 26.6 us  [on_device(): lax.ppermute(ring[-1], 'tp', [(dev, (dev + 1) % 4) for dev in range(4)])]
    all_gather x1, waiting for transfers between devices: 178 us -> 161 us  [on_device(): lax.all_gather(out_weight, 'seq', axis=1, tiled=True)]
    unnamed x46 -> x54, local copies, waits for them, and re-layouts: 19.6 us -> 22.9 us
  transfers between devices with their start and end apart: 6 -> 8, of which waited for: 5 -> 5; matrix products, arithmetic and copies ran while one was open for 16% -> 18% of each run, Pallas kernels for 0% -> 0%
where the time goes in v1:
time: 639 us; the launch traced here: 630 us
  waiting for transfers between devices  415 us (65%)
  matrix products  92.7 us (15%)
  local copies, waits for them, and re-layouts  55 us (9%)
  other arithmetic  24.8 us (4%)
  blocking collectives  21.7 us (3%)
  between operations  14.5 us (2%)
    all_to_all x1, waiting for transfers between devices, on_device(): lax.all_to_all(cotangent, 'seq', split_axis=1, concat_axis=0, tiled=True)  193 us
    all_gather x1, waiting for transfers between devices, on_device(): lax.all_gather(out_weight, 'seq', axis=1, tiled=True)  161 us
    all_gather x1, waiting for transfers between devices, on_device(): lax.all_gather(normed, 'seq', axis=0, tiled=True)  33.6 us
    ppermute x3, waiting for transfers between devices, on_device(): lax.ppermute(ring[-1], 'tp', [(dev, (dev + 1) % 4) for dev in range(4)])  26.6 us
    unnamed x54, local copies, waits for them, and re-layouts  22.9 us
    all_gather x1, blocking collectives, carried_in(): pieces = jax.tree.map(lambda part: lax.all_gather(part, axis), value)  21.7 us
    select_n x14, other arithmetic, turn(): jnp.where(position < mine, new, old)  16.9 us
  transfers between devices with their start and end apart: 8, of which 5 were waited for; matrix products, arithmetic and copies ran while one was open for 18% of the time, Pallas kernels for 0%

profile of v1, /device:TPU:0, one launch (start us, length us, event | category | flops | bytes accessed | tf_op | source)
XLA Modules:
  0.0 629.7 jit_solution(6949188642259650296)
XLA Ops:
  18.2 4.5 fusion.47
  24.7 20.2 %collective-permute-done = bf16[512,1536]{0,1:T(8,128)(2,1)} collective-permute-done((bf16[512,1536]{0,1:T(8,128)(2,1)S(1)}, bf16[512,1536]{0,1:T(8,128)(2,1)}, u32[]{:S(2)}, u32[]{:S(2)}) %collective-permute-start) | collective-permute-done | bytes 1572896 | tf_op jit(solution)/shard_map/ppermute | solution.py:89
  49.5 21.7 %all-gather.2 = f32[8,1,8]{2,1,0:T(1,128)S(1)} all-gather(f32[1,1,8]{2,1,0:T(1,128)S(1)} %get-tuple-element.258), channel_id=1, replica_groups=mesh['seq'=8,'tp'=4] {'seq'}, dimensions={0}, use_global_device_ids=true | all-gather | bytes 288 | tf_op jit(solution)/shard_map/all_gather | solution.py:13
  71.3 6.4 %fusion.49 = f32[8,128,128,2]{2,3,1,0:T(2,128)} fusion(f32[2,8,128,128]{3,2,1,0:T(8,128)} %copy-done.19, pred[2,2]{1,0:T(4,128)(4,1)S(1)} %iota_compare_fusion.2, f32[2,8]{0,1:T(8,128)S(1)} %copy.183, f32[2,8]{0,1:T(8,128)S(1)} %bitcast.169), kind=kOutput, calls=%fused_computation.65 | convolution fusion | flops 6291552 | bytes 2097284 | tf_op jit(solution)/shard_map/nmh,mhde->nhde/dot_general | solution.py:72
  79.7 5.0 fusion.6
  84.7 6.5 %collective-permute-done.2 = bf16[512,1536]{0,1:T(8,128)(2,1)S(1)} collective-permute-done((bf16[512,1536]{0,1:T(8,128)(2,1)}, bf16[512,1536]{0,1:T(8,128)(2,1)S(1)}, u32[]{:S(2)}, u32[]{:S(2)}) %collective-permute-start.2) | collective-permute-done | bytes 1572896 | tf_op jit(solution)/shard_map/ppermute | solution.py:89
  97.7 4.3 constant_dynamic-slice_fusion
  102.0 8.8 %while.28 = (s32[]{:T(128)}, f32[8,128,128]{2,1,0:T(8,128)S(1)}, s32[]{:T(128)}, f32[8,8]{1,0:T(8,128)S(1)}, f32[8,8,128,128]{3,2,1,0:T(8,128)}, /*index=5*/s32[]{:T(128)}, s32[]{:T(128)}) while((s32[]{:T(128)}, f32[8,128,128]{2,1,0:T(8,128)S(1)}, s32[]{:T(128)}, f32[8,8]{1,0:T(8,128)S(1)}, f32[8,8,128,128]{3,2,1,0:T(8,128)}, ...), condition=%wide.region_4.5_spmd.clone, body=%wide.region_3.4_spmd.clone.sunk | while | flops 524292 | bytes 1573065 | solution.py:25
  110.8 3.6 multiply_reduce_fusion.1
  114.4 161.2 %all-gather.8.cloned.1.call-done = bf16[1024,6144]{1,0:T(8,128)(2,1)} async-done(((bf16[1024,768]{1,0:T(8,128)(2,1)}), bf16[1024,6144]{1,0:T(8,128)(2,1)}) %all-gather.8.cloned.1.call-update) | async-done | bytes 12582928 | tf_op jit(solution)/shard_map/all_gather | solution.py:95
  275.7 11.5 %convolution_bitcast_fusion = f32[64,8,8,128]{3,1,2,0:T(8,128)S(1)} fusion(bf16[512,6144]{0,1:T(8,128)(2,1)} %constant_dynamic-slice_fusion, bf16[1024,6144]{1,0:T(8,128)(2,1)} %all-gather.8.cloned.1.call-done), kind=kOutput, calls=%fused_computation.49 | convolution fusion | flops 6442450944 | bytes 20971520 | tf_op jit(solution)/shard_map/dot_general | solution.py:93
  300.8 4.4 fusion.43
  305.3 4.8 all-to-all-start
  315.2 192.9 %all-to-all-done = bf16[512,8,768]{0,2,1:T(8,128)(2,1)} async-done(((bf16[512,8,768]{0,2,1:T(8,128)(2,1)}), bf16[512,8,768]{0,2,1:T(8,128)(2,1)}, u32[]{:S(2)}, u32[]{:S(2)}) %all-to-all-start) | async-done | bytes 6291488 | tf_op jit(solution)/shard_map/all_to_all | solution.py:125
  508.2 8.7 %copy.212 = bf16[8,512,768]{2,1,0:T(8,128)(2,1)} copy(bf16[8,512,768]{1,2,0:T(8,128)(2,1)} %bitcast.34) | data formatting | bytes 12582912 | tf_op jit(solution)/shard_map/all_to_all | solution.py:125
  516.8 3.2 fusion.53
  520.1 3.7 fusion.10
  532.4 6.3 %fusion.45 = f32[8,128,128,2]{2,3,1,0:T(2,128)} fusion(f32[2,8,128,128]{3,2,1,0:T(8,128)} %copy-done.17, pred[2,2]{1,0:T(4,128)(4,1)S(1)} %iota_compare_fusion.1, f32[2,8]{0,1:T(8,128)S(1)} %copy.183, f32[2,8]{0,1:T(8,128)S(1)} %copy.200), kind=kOutput, calls=%fused_computation.61 | convolution fusion | flops 6291552 | bytes 2097284 | tf_op jit(solution)/shard_map/nmh,mhde->nhde/dot_general | solution.py:113
  538.7 8.0 %fusion.8 = f32[2,8,256,128]{3,2,1,0:T(8,128)} fusion(bf16[2,256,8,128]{1,3,2,0:T(8,128)(2,1)S(1)} %copy-done.6, f32[2,8,256,256]{3,2,1,0:T(8,128)} %copy-done.16, f32[2,8,256]{2,1,0:T(8,128)S(1)} %add_bitcast_fusion.1, pred[256,256]{1,0:T(8,128)(4,1)S(1)} %iota_compare_fusion), kind=kOutput, calls=%fused_computation.11 | convolution fusion | flops 1614807040 | bytes 7421952 | tf_op jit(solution)/shard_map/nhts,nthd->nshd/dot_general | solution.py:117
  546.7 9.2 %fusion.4 = f32[2,8,128,256]{2,3,1,0:T(8,128)} fusion(f32[2,256,8,128]{1,3,2,0:T(8,128)S(1)} %get-tuple-element.255, f32[2,8,256,256]{3,2,1,0:T(8,128)S(1)} %copy-done.3, f32[2,8,256]{2,1,0:T(8,128)S(1)} %add_bitcast_fusion.1, pred[256,256]{1,0:T(8,128)(4,1)S(1)} %iota_compare_fusion), kind=kOutput, calls=%fused_computation.9 | convolution fusion | flops 1614807040 | bytes 8470528 | tf_op jit(solution)/shard_map/nhts,nthe->nshe/dot_general | solution.py:121
  555.9 4.8 rev.7
  560.7 8.6 %while.29 = (s32[]{:T(128)}, f32[8,128,128]{2,1,0:T(8,128)S(1)}, s32[]{:T(128)}, f32[8,8]{1,0:T(8,128)S(1)}, f32[8,8,128,128]{3,2,1,0:T(8,128)}, /*index=5*/s32[]{:T(128)}, s32[]{:T(128)}) while((s32[]{:T(128)}, f32[8,128,128]{2,1,0:T(8,128)S(1)}, s32[]{:T(128)}, f32[8,8]{1,0:T(8,128)S(1)}, f32[8,8,128,128]{3,2,1,0:T(8,128)}, ...), condition=%wide.region_8.9_spmd.clone, body=%wide.region_7.8_spmd.clone.sunk | while | flops 524292 | bytes 1573065 | solution.py:25
  577.3 33.6 %all-gather.10.cloned.1.call-done = bf16[4096,1024]{1,0:T(8,128)(2,1)} async-done(((bf16[512,1024]{1,0:T(8,128)(2,1)}), bf16[4096,1024]{1,0:T(8,128)(2,1)}) %all-gather.10.cloned.1.call-update) | async-done | bytes 8388624 | tf_op jit(solution)/shard_map/all_gather | solution.py:128
  610.9 12.1 %fusion.95 = f32[768,1024]{1,0:T(8,128)} fusion(bf16[4096,768]{1,0:T(8,128)(2,1)} %bitcast.154, bf16[4096,1024]{1,0:T(8,128)(2,1)} %all-gather.10.cloned.1.call-done), kind=kOutput, calls=%fused_computation.135 | convolution fusion | flops 6442450944 | bytes 17825792 | tf_op jit(solution)/shard_map/dot_general | solution.py:126
  (139 shorter events, 78.3 us)
Async XLA Ops:
  7.2 94.8 %all-gather.12.cloned.1.call-start = ((), (), s32[]{:S(2)}) async-start(), calls=%async_computation.3 | async-start | bytes 4718592 | tf_op jit(solution)/shard_map/all_gather | solution.py:13
  13.5 10.0 %copy-start.18 = (bf16[512,1536]{1,0:T(8,128)(2,1)S(1)}, bf16[512,1536]{1,0:T(8,128)(2,1)}, u32[]{:S(2)}) copy-start(bf16[512,1536]{1,0:T(8,128)(2,1)} %param.15) | copy-start | bytes 4718596
  22.7 253.0 %all-gather.8.cloned.1.call-start = ((), (), s32[]{:S(2)}) async-start(), calls=%async_computation.1 | async-start | bytes 14155776 | tf_op jit(solution)/shard_map/all_gather | solution.py:95
  23.4 532.5 %all-gather.14.cloned.1.call-start = ((), (), s32[]{:S(2)}) async-start(), calls=%async_computation.4 | async-start | bytes 4718592 | tf_op jit(solution)/shard_map/all_gather | solution.py:13
  24.2 20.7 %collective-permute-start = (bf16[512,1536]{0,1:T(8,128)(2,1)S(1)}, bf16[512,1536]{0,1:T(8,128)(2,1)}, u32[]{:S(2)}, u32[]{:S(2)}) collective-permute-start(bf16[512,1536]{0,1:T(8,128)(2,1)S(1)} %copy.172), channel_id=1, source_target_pairs={{0,1},{1,2},{2,3},{3,0},{4,5},{5,6},{6,7},{7,4},{8,9},{9,10},{10,1... | collective-permute-start | bytes 4718600 | tf_op jit(solution)/shard_map/ppermute | solution.py:89
  44.9 26.3 %collective-permute-start.1 = (bf16[512,1536]{0,1:T(8,128)(2,1)}, bf16[512,1536]{0,1:T(8,128)(2,1)}, u32[]{:S(2)}, u32[]{:S(2)}) collective-permute-start(bf16[512,1536]{0,1:T(8,128)(2,1)} %collective-permute-done), channel_id=1, source_target_pairs={{0,1},{1,2},{2,3},{3,0},{4,5},{5,6},{6,7},{7,4},{8,9},{9,10},{10,1... | collective-permute-start | bytes 4718600 | tf_op jit(solution)/shard_map/ppermute | solution.py:89
  49.4 30.3 %copy-start.4 = (bf16[2,256,8,128]{1,3,2,0:T(8,128)(2,1)}, bf16[2,256,8,128]{1,3,2,0:T(8,128)(2,1)S(1)}, u32[]{:S(2)}) copy-start(bf16[2,256,8,128]{1,3,2,0:T(8,128)(2,1)S(1)} %copy.198) | copy-start | bytes 3145732
  71.2 20.1 %collective-permute-start.2 = (bf16[512,1536]{0,1:T(8,128)(2,1)}, bf16[512,1536]{0,1:T(8,128)(2,1)S(1)}, u32[]{:S(2)}, u32[]{:S(2)}) collective-permute-start(bf16[512,1536]{0,1:T(8,128)(2,1)} %collective-permute-done.1), channel_id=1, source_target_pairs={{0,1},{1,2},{2,3},{3,0},{4,5},{5,6},{6,7},{7,4},{8,9},{9,10},{10,1... | collective-permute-start | bytes 4718600 | tf_op jit(solution)/shard_map/ppermute | solution.py:89
  71.3 8.4 %copy-start.9 = (bf16[64,8,8,128]{3,2,1,0:T(8,128)(2,1)S(1)}, bf16[64,8,8,128]{3,2,1,0:T(8,128)(2,1)}, u32[]{:S(2)}) copy-start(bf16[64,8,8,128]{3,2,1,0:T(8,128)(2,1)} %copy-done.8) | copy-start | bytes 3145732
  79.7 5.1 copy-start.2
  114.4 177.8 %copy-start = (f32[2,256,8,128]{1,3,2,0:T(8,128)}, f32[2,256,8,128]{1,3,2,0:T(8,128)S(1)}, u32[]{:S(2)}) copy-start(f32[2,256,8,128]{1,3,2,0:T(8,128)S(1)} %get-tuple-element.260) | copy-start | bytes 6291460
  292.2 2.2 copy-start.1
  294.4 3.2 copy-start.5
  305.3 202.9 %all-to-all-start = ((bf16[512,8,768]{0,2,1:T(8,128)(2,1)}), bf16[512,8,768]{0,2,1:T(8,128)(2,1)}, u32[]{:S(2)}, u32[]{:S(2)}) async-start(bf16[512,8,768]{0,2,1:T(8,128)(2,1)} %bitcast.144), calls=%async_computation | async-start | bytes 12582912 | tf_op jit(solution)/shard_map/all_to_all | solution.py:125
  310.1 300.8 %all-gather.10.cloned.1.call-start = ((), (), s32[]{:S(2)}) async-start(), calls=%async_computation.2 | async-start | bytes 9437184 | tf_op jit(solution)/shard_map/all_gather | solution.py:128
  516.8 3.2 copy-start.12
  520.1 3.7 copy-start.16
  520.1 3.7 copy-start.14
  529.9 8.9 %copy-start.6 = (bf16[2,256,8,128]{1,3,2,0:T(8,128)(2,1)S(1)}, bf16[2,256,8,128]{1,3,2,0:T(8,128)(2,1)}, u32[]{:S(2)}) copy-start(bf16[2,256,8,128]{1,3,2,0:T(8,128)(2,1)} %copy-done.4) | copy-start | bytes 3145732
  538.7 8.0 %copy-start.3 = (f32[2,8,256,256]{3,2,1,0:T(8,128)S(1)}, f32[2,8,256,256]{3,2,1,0:T(8,128)}, u32[]{:S(2)}) copy-start(f32[2,8,256,256]{3,2,1,0:T(8,128)} %copy-done.2) | copy-start | bytes 12582916
  555.9 13.4 %copy-start.10 = (bf16[64,8,8,128]{3,2,1,0:T(8,128)(2,1)S(1)}, bf16[64,8,8,128]{3,2,1,0:T(8,128)(2,1)}, u32[]{:S(2)}) copy-start(bf16[64,8,8,128]{3,2,1,0:T(8,128)(2,1)} %copy-done.8) | copy-start | bytes 3145732
  560.7 8.6 %copy-start.7 = (f32[8,128,128,2]{2,3,1,0:T(2,128)S(1)}, f32[8,128,128,2]{2,3,1,0:T(2,128)}, u32[]{:S(2)}) copy-start(f32[8,128,128,2]{2,3,1,0:T(2,128)} %fusion.45) | copy-start | bytes 3145732
  569.3 3.7 copy-start.13
  569.3 3.7 copy-start.15
  (4 other events, 4.8 us)
Sparse Core Ops, SparseCore 0:
  22.8 76.1 all-gather.11
  101.1 174.4 all-gather.7
  305.4 177.9 all-gather.13
  485.4 125.4 all-gather.9
